TPU v7x, 512 devices: a whole 4x4x16 slice. The times are simulated.
512 devices in a mesh: clips: 32 (over y, x, core), slab: 16 (over z).
Axes of the slice: x: 4, y: 4, z: 16, core: 2. Of those that a mesh axis runs over, the one named last changes fastest.
Arguments:
- video: bfloat16 [64, 6, 16, 16, 256], P('clips', None, 'slab'), may hold values from -6 to 6
- clip_blocks: int32 [64], replicated, may hold values from 1 to 3, 128 in all
- deal_order: int32 [32], replicated, may hold values from 0 to 31, each once
- kernel: bfloat16 [256, 3456], P('clips', 'slab'), may hold values from -0.078125 to 0.078125
- gain: float32 [128], replicated, may hold values from 0.25 to 1.75
- bias: float32 [128], replicated, may hold values from -3 to 3
- cotangent: bfloat16 [128, 2, 16, 16, 128], P('clips', None, 'slab'), may hold values from -6 to 6
Outputs:
- activations: bfloat16 [128, 2, 16, 16, 128], P('clips', None, 'slab')
- video_grad: bfloat16 [64, 6, 16, 16, 256], P('clips', None, 'slab')
- kernel_grad: float32 [256, 3456], P('clips', 'slab')
- gain_grad: float32 [128], replicated
- bias_grad: float32 [128], replicated
Inputs may be any that keep to these rules, and one draw needn't show every extreme that they name: `clip_blocks`: the blocks of all clips add up to 4 times the number of devices along clips, so every device receives exactly 4 blocks; some clip has 3 blocks. `deal_order`: a permutation of the devices along clips.
All inputs are finite; a program needn't handle non-finite values.
Results may differ from a plain program's by a relative error of at most 0.0049.
Values may be sent and summed in bfloat16 or wider, within the bound.
A program may use at most 64 MiB of HBM per device.

v0:
```python
import jax
import jax.numpy as jnp
from jax import lax
from jax.sharding import PartitionSpec as P

GROUPS = 16
TAPS = 27
FB = 2
BMAX = 3


def extended(array, sides, width):
    for axis, dim in sides:
        size, length = (lax.axis_size(axis), array.shape[dim])
        up = [(i, (i + 1) % size) for i in range(size - 1)]
        down = [(j, i) for i, j in up]
        last = lax.slice_in_dim(array, length - width, length, axis=dim)
        initial = lax.slice_in_dim(array, 0, width, axis=dim)
        before = lax.ppermute(last, axis, up)
        after = lax.ppermute(initial, axis, down)
        array = jnp.concatenate([before, array, after], axis=dim)
    return array


def body(video, clip_blocks, deal_order, kernel, gain, bias, cotangent):
    clip_devs = lax.axis_size("clips")
    slab_devs = lax.axis_size("slab")
    own_index = lax.axis_index("clips")
    held_clips, frame_count, row_count, column_count, in_channels = video.shape
    slot_count = cotangent.shape[0]
    out_channels = gain.shape[0]
    all_clips = clip_blocks.shape[0]
    per_group = out_channels // GROUPS
    capacity = -(-(held_clips * BMAX) // clip_devs)
    block_ends = jnp.cumsum(clip_blocks)
    block_starts = block_ends - clip_blocks
    device_ids = jnp.arange(clip_devs, dtype=jnp.int32)
    deal_slot = jnp.sum(
        jnp.where(deal_order[:, None] == device_ids[None, :], device_ids[:, None], 0), axis=0
    )
    first_clip = own_index * held_clips
    own_start = block_starts[first_clip]
    own_end = block_ends[first_clip + held_clips - 1]
    dest_rank = jnp.repeat(device_ids, capacity)
    turn_index = jnp.tile(jnp.arange(capacity, dtype=jnp.int32), clip_devs)
    slot_blocks = jnp.arange(slot_count, dtype=jnp.int32) * clip_devs + deal_slot[own_index]

    def clip_index(block_id):
        return jnp.sum((block_ends <= block_id[..., None]).astype(jnp.int32), axis=-1)

    full_kernel = lax.all_gather(kernel, "slab", axis=1, tiled=True)
    full_kernel = lax.all_gather(full_kernel, "clips", axis=0, tiled=True)
    kernel_taps = full_kernel.reshape(in_channels, out_channels, TAPS).transpose(2, 0, 1)

    def group_sums(values):
        return jnp.sum(values.reshape(values.shape[:4] + (GROUPS, per_group)), axis=(1, 2, 3, 5))

    def spread(stat):
        return stat[:, None, None, None, :, None]

    cells_clip = FB * row_count * slab_devs * column_count * per_group
    context_video = jnp.pad(video, ((0, 0), (2, 0), (0, 0), (0, 0), (0, 0)))
    highest = lax.Precision.HIGHEST
    first_block = own_start + jnp.mod(deal_slot[dest_rank] - own_start, clip_devs)
    block_id = first_block + turn_index * clip_devs
    is_live = block_id < own_end
    clip_global = jnp.minimum(clip_index(block_id), all_clips - 1)
    clip_local = jnp.clip(clip_global - first_clip, 0, held_clips - 1)
    block_local = jnp.clip(block_id - block_starts[clip_global], 0, BMAX - 1)
    window = FB + 2

    def window_of(clip_pick, block_pick):
        begin = (clip_pick, block_pick * FB, 0, 0, 0)
        sizes = (1, window, row_count, column_count, context_video.shape[-1])
        return lax.dynamic_slice(context_video, begin, sizes)[0]

    pieces = jax.vmap(window_of)(clip_local, block_local)
    pieces = jnp.where(
        is_live[:, None, None, None, None], pieces, jnp.zeros((), context_video.dtype)
    )
    sent = pieces.reshape((clip_devs, capacity) + pieces.shape[1:])
    received = lax.all_to_all(sent, "clips", split_axis=0, concat_axis=0, tiled=True)
    clip_global = clip_index(slot_blocks)
    source_rank = clip_global // held_clips
    turn_of = (slot_blocks - block_starts[source_rank * held_clips]) // clip_devs
    flat_rows = received.reshape((clip_devs * capacity,) + received.shape[2:])
    input_slots = flat_rows[source_rank * capacity + turn_of]
    rimmed = extended(input_slots, (("slab", 2),), 1)
    padded = jnp.pad(rimmed, ((0, 0), (0, 0), (0, 0), (1, 1), (0, 0)))
    forward_outputs = input_slots.shape[1] - 2
    totals = jnp.zeros(
        (input_slots.shape[0] * forward_outputs * row_count * column_count, out_channels),
        jnp.float32,
    )
    for forward_step_a in range(3):
        for forward_step_b in range(3):
            for forward_step_c in range(3):
                tap_rows = padded[
                    :,
                    forward_step_a : forward_step_a + forward_outputs,
                    forward_step_b : forward_step_b + row_count,
                    forward_step_c : forward_step_c + column_count,
                    :,
                ].reshape(-1, in_channels)
                totals = totals + jnp.dot(
                    tap_rows,
                    kernel_taps[(forward_step_a * 3 + forward_step_b) * 3 + forward_step_c],
                    preferred_element_type=jnp.float32,
                )
    conv_out = totals.reshape(
        input_slots.shape[0], forward_outputs, row_count, column_count, out_channels
    )
    slot_clip = clip_index(slot_blocks)
    chooser = (slot_clip[:, None] == jnp.arange(all_clips, dtype=jnp.int32)[None, :]).astype(
        jnp.float32
    )
    table_first = jnp.dot(chooser.T, group_sums(conv_out), precision=highest)
    table_second = jnp.dot(chooser.T, group_sums(conv_out * conv_out), precision=highest)
    table_first, table_second = lax.psum((table_first, table_second), ("clips", "slab"))
    counts = (clip_blocks * cells_clip).astype(jnp.float32)
    group_mean = table_first / counts[:, None]
    group_var = table_second / counts[:, None] - group_mean * group_mean
    clip_mean = group_mean
    clip_inv = lax.rsqrt(group_var + 1e-05)
    group_mean = jnp.dot(chooser, clip_mean, precision=highest)
    inv_std = jnp.dot(chooser, clip_inv, precision=highest)
    grouped = conv_out.reshape(conv_out.shape[:4] + (GROUPS, per_group))
    normed = ((grouped - spread(group_mean)) * spread(inv_std)).reshape(conv_out.shape)
    affine = normed * gain + bias
    activations = jax.nn.silu(affine).astype(jnp.bfloat16)
    sigmoid = jax.nn.sigmoid(affine)
    grad_affine = cotangent.astype(jnp.float32) * sigmoid * (1.0 + affine * (1.0 - sigmoid))
    gain_part = jnp.sum(grad_affine * normed, axis=(0, 1, 2, 3))
    bias_part = jnp.sum(grad_affine, axis=(0, 1, 2, 3))
    grad_normed, gain_part, bias_part = (grad_affine * gain, gain_part, bias_part)
    sum_grad = jnp.dot(chooser.T, group_sums(grad_normed), precision=highest)
    sum_cross = jnp.dot(chooser.T, group_sums(grad_normed * normed), precision=highest)
    sum_grad, sum_cross, gain_grad, bias_grad = lax.psum(
        (sum_grad, sum_cross, gain_part, bias_part), ("clips", "slab")
    )
    mean_grad = jnp.dot(chooser, sum_grad / counts[:, None], precision=highest)
    mean_cross = jnp.dot(chooser, sum_cross / counts[:, None], precision=highest)
    grouped = grad_normed.reshape(grad_normed.shape[:4] + (GROUPS, per_group))
    normed_groups = normed.reshape(grouped.shape)
    result = spread(inv_std) * (grouped - spread(mean_grad) - normed_groups * spread(mean_cross))
    grad_conv = result.reshape(grad_normed.shape).astype(jnp.bfloat16)
    range_start = block_starts[dest_rank * held_clips]
    range_end = block_ends[dest_rank * held_clips + held_clips - 1]
    first_block = range_start + jnp.mod(deal_slot[own_index] - range_start, clip_devs)
    block_id = first_block + turn_index * clip_devs
    is_live = block_id < range_end
    slot_index = jnp.clip(block_id // clip_devs, 0, slot_count - 1)
    pieces = jnp.where(
        is_live[:, None, None, None, None], grad_conv[slot_index], jnp.zeros((), grad_conv.dtype)
    )
    returned = lax.all_to_all(
        pieces.reshape((clip_devs, capacity) + pieces.shape[1:]),
        "clips",
        split_axis=0,
        concat_axis=0,
        tiled=True,
    )
    clip_global = first_clip + jnp.arange(held_clips, dtype=jnp.int32)[:, None]
    block_range = jnp.arange(BMAX, dtype=jnp.int32)[None, :]
    block_id = block_starts[clip_global] + block_range
    is_live = block_range < clip_blocks[clip_global]
    source_rank = deal_order[jnp.mod(block_id, clip_devs)]
    turn_of = (block_id - own_start) // clip_devs
    row_index = jnp.where(is_live, source_rank * capacity + turn_of, 0)
    flat_rows = returned.reshape((clip_devs * capacity,) + returned.shape[2:])
    pieces = jnp.where(
        is_live[:, :, None, None, None, None], flat_rows[row_index], jnp.zeros((), returned.dtype)
    )
    grad_clip = pieces.reshape((held_clips, frame_count) + pieces.shape[3:])
    rimmed_grad = extended(grad_clip, (("slab", 2),), 1)
    grad_padded = jnp.pad(rimmed_grad, ((0, 0), (0, 2), (0, 0), (1, 1), (0, 0)))
    totals = jnp.zeros(
        (held_clips * frame_count * row_count * column_count, in_channels), jnp.float32
    )
    for step_a in range(3):
        for step_b in range(3):
            for step_c in range(3):
                moved = grad_padded[
                    :,
                    2 - step_a : 2 - step_a + frame_count,
                    2 - step_b : 2 - step_b + row_count,
                    2 - step_c : 2 - step_c + column_count,
                    :,
                ].reshape(-1, out_channels)
                totals = totals + lax.dot_general(
                    moved,
                    kernel_taps[(step_a * 3 + step_b) * 3 + step_c],
                    (((1,), (1,)), ((), ())),
                    preferred_element_type=jnp.float32,
                )
    video_grad = totals.reshape(video.shape).astype(jnp.bfloat16)
    outputs = grad_conv.shape[1]
    grad_flat = grad_conv.reshape(-1, out_channels)
    take_count = in_channels // clip_devs * lax.axis_size("clips")
    tap_parts = []
    for step_a in range(3):
        for step_b in range(3):
            for step_c in range(3):
                tap_rows = padded[
                    :,
                    step_a : step_a + outputs,
                    step_b : step_b + row_count,
                    step_c : step_c + column_count,
                    :,
                ].reshape(-1, take_count)
                tap_parts.append(
                    lax.dot_general(
                        tap_rows,
                        grad_flat,
                        (((0,), (0,)), ((), ())),
                        preferred_element_type=jnp.float32,
                    )
                )
    partial_grad = lax.psum_scatter(
        jnp.stack(tap_parts, axis=2).reshape(take_count, out_channels * TAPS),
        "clips",
        scatter_dimension=0,
        tiled=True,
    )
    kernel_grad = lax.psum_scatter(partial_grad, "slab", scatter_dimension=1, tiled=True)
    return (activations, video_grad, kernel_grad, gain_grad, bias_grad)


def solution(mesh):
    return jax.shard_map(
        body,
        mesh=mesh,
        in_specs=(
            P("clips", None, "slab", None, None),
            P(),
            P(),
            P("clips", "slab"),
            P(),
            P(),
            P("clips", None, "slab", None, None),
        ),
        out_specs=(
            P("clips", None, "slab", None, None),
            P("clips", None, "slab", None, None),
            P("clips", "slab"),
            P(),
            P(),
        ),
        check_vma=False,
    )
```

profile of v0, /device:TPU:2, one launch (start us, length us, event | category | flops | bytes accessed | tf_op | source)
XLA Modules:
  0.0 642.9 jit_solution(1696978957917538280)
XLA Ops:
  9.0 1.2 multiply_convert_fusion.2
  12.8 1.3 broadcast_compare_fusion
  16.4 1.1 fusion.36
  17.6 9.5 %all-to-all-start = ((bf16[32,1,4,1,16,256]{5,4,2,3,1,0:T(8,128)(2,1)}), bf16[32,1,4,1,16,256]{5,4,2,3,1,0:T(8,128)(2,1)S(1)}, u32[]{:S(2)}, u32[]{:S(2)}) async-start(bf16[32,1,4,1,16,256]{5,4,2,3,1,0:T(8,128)(2,1)} %fusion.36), calls=%async_computation | async-start | bytes 2097152 | tf_op jit(solution)/shard_map/all_to_all | solution.py:82
  27.1 33.9 %all-gather = bf16[16,216,8]{1,2,0:T(8,128)(2,1)S(1)} all-gather(bf16[1,216,8]{1,2,0:T(8,128)(2,1)S(1)} %bitcast.755), channel_id=1, replica_groups=mesh['clips'=32,'slab'=16] {'slab'}, dimensions={0}, use_global_device_ids=true | all-gather | bytes 58752 | tf_op jit(solution)/shard_map/all_gather | solution.py:51
  69.1 1.3 dynamic-slice.1
  73.7 1.3 collective-permute-start.1
  75.0 4.6 collective-permute-start
  80.5 1.5 collective-permute-done
  83.7 1.0 fusion.226
  84.7 31.1 %all-gather.3.cloned.1.call-done = bf16[256,3456]{1,0:T(8,128)(2,1)} async-done(((bf16[8,3456]{1,0:T(8,128)(2,1)}), bf16[256,3456]{1,0:T(8,128)(2,1)}) %all-gather.3.cloned.1.call-update) | async-done | bytes 1769488 | tf_op jit(solution)/shard_map/all_gather | solution.py:52
  115.8 3.9 copy.95
  119.6 2.6 reshape.1229
  122.2 3.5 fusion.224
  125.7 1.8 fusion.225
  127.5 1.1 copy.122
  128.6 1.0 copy.116
  129.7 1.0 copy.113
  131.0 1.0 copy.96
  132.0 1.0 copy.97
  133.1 1.0 copy.98
  134.1 1.0 copy.99
  135.1 1.0 copy.100
  136.2 1.0 copy.101
  137.2 1.0 copy.102
  138.3 1.0 copy.103
  139.3 1.0 copy.105
  140.3 1.0 copy.106
  141.4 1.0 copy.108
  142.4 1.0 copy.109
  143.4 1.0 copy.110
  144.6 1.0 copy.112
  146.7 1.0 fusion.81
  148.7 1.0 fusion.102
  149.7 1.0 fusion.115
  151.0 1.0 convolution_add_fusion.44
  152.0 1.0 convolution_add_fusion.43
  153.0 1.0 convolution_add_fusion.42
  154.0 1.0 convolution_add_fusion.41
  155.0 1.0 convolution_add_fusion.40
  156.0 1.0 convolution_add_fusion.39
  157.0 1.0 fusion.35
  158.0 1.0 convolution_add_fusion.37
  159.0 1.0 fusion.34
  160.0 1.0 convolution_add_fusion.35
  161.0 1.0 convolution_add_fusion.34
  162.0 1.0 convolution_add_fusion.33
  163.0 1.0 convolution_add_fusion.32
  164.0 1.0 fusion.33
  165.0 1.0 convolution_add_fusion.30
  166.0 1.0 fusion.32
  167.1 1.0 convolution_add_fusion.27
  171.3 104.3 %all-reduce.6 = (f32[64,16]{0,1:T(8,128)S(1)}, f32[64,16]{0,1:T(8,128)S(1)}) all-reduce(f32[64,16]{0,1:T(8,128)S(1)} %fusion.160, f32[64,16]{0,1:T(8,128)S(1)} %fusion.161), channel_id=1, replica_groups=mesh['clips'=32,'slab'=16] {'clips','slab'}, use_global_device_ids=true, to_apply=%region_7.8 | all-reduce | flops 2048 | bytes 16384 | tf_op jit(solution)/shard_map/psum | solution.py:119
  277.8 100.7 %all-reduce.5 = (f32[64,16]{0,1:T(8,128)S(1)}, f32[64,16]{0,1:T(8,128)S(1)}, f32[128]{0:T(128)}, f32[128]{0:T(128)}) all-reduce(f32[64,16]{0,1:T(8,128)S(1)} %fusion.158, f32[64,16]{0,1:T(8,128)S(1)} %fusion.159, f32[128]{0:T(128)S(1)} %get-tuple-element.25, ...), channel_id=1, replica_groups=mesh['clips'=32,'slab'=16] {'clips','slab'}, use_global_device_ids=true, to_apply=%region_13.14 | all-reduce | flops 2304 | bytes 18432 | tf_op jit(solution)/shard_map/psum | solution.py:138
  381.6 5.0 all-to-all-start.1
  409.2 6.0 copy.126
  415.3 4.9 reshape.1311
  420.9 1.3 collective-permute-start.3
  422.2 4.5 collective-permute-start.2
  426.9 1.6 collective-permute-done.2
  433.5 124.2 %all-reduce.9.cloned.1.call-done = f32[256,3456]{0,1:T(8,128)} async-done(((f32[256,3456]{0,1:T(8,128)}), f32[256,3456]{0,1:T(8,128)}) %all-reduce.9.cloned.1.call-update) | async-done | bytes 3538960
  557.7 3.2 constant_dynamic-slice_fusion
  561.8 73.0 %reduce-scatter.5.cloned.1.call-done = f32[8,216]{0,1:T(8,128)} async-done(((f32[8,3456]{0,1:T(8,128)}), f32[8,216]{0,1:T(8,128)}) %reduce-scatter.5.cloned.1.call-update) | async-done | bytes 6928
  634.8 1.6 copy.128
  (215 shorter events, 60.4 us)
Async XLA Ops:
  14.2 12.8 %copy-start.15 = (bf16[8,216]{1,0:T(8,128)(2,1)S(1)}, bf16[8,216]{1,0:T(8,128)(2,1)}, u32[]{:S(2)}) copy-start(bf16[8,216]{1,0:T(8,128)(2,1)} %param.10) | copy-start | bytes 10372
  15.7 46.8 %copy-start.1 = (s32[64]{0:T(128)S(1)}, s32[64]{0:T(128)}, u32[]{:S(2)}) copy-start(s32[64]{0:T(128)} %param.8) | copy-start | bytes 772
  15.7 48.2 %copy-start = (s32[32]{0:T(128)S(1)}, s32[32]{0:T(128)}, u32[]{:S(2)}) copy-start(s32[32]{0:T(128)} %param.9) | copy-start | bytes 388
  17.6 55.5 %all-to-all-start = ((bf16[32,1,4,1,16,256]{5,4,2,3,1,0:T(8,128)(2,1)}), bf16[32,1,4,1,16,256]{5,4,2,3,1,0:T(8,128)(2,1)S(1)}, u32[]{:S(2)}, u32[]{:S(2)}) async-start(bf16[32,1,4,1,16,256]{5,4,2,3,1,0:T(8,128)(2,1)} %fusion.36), calls=%async_computation | async-start | bytes 2097152 | tf_op jit(solution)/shard_map/all_to_all | solution.py:82
  27.0 88.8 %all-gather.3.cloned.1.call-start = ((), (), s32[]{:S(2)}) async-start(), calls=%async_computation.3 | async-start | bytes 1824768 | tf_op jit(solution)/shard_map/all_gather | solution.py:52
  65.5 8.2 %copy-start.20 = (s32[4]{0:T(128)}, s32[4]{0:T(128)S(1)}, u32[]{:S(2)}) copy-start(s32[4]{0:T(128)S(1)} %convert_reduce_fusion.1) | copy-start | bytes 52
  73.7 6.9 %collective-permute-start.1 = (bf16[4,4,1,16,256]{4,3,1,0,2:T(8,128)(2,1)S(1)}, bf16[4,4,1,16,256]{4,3,1,0,2:T(8,128)(2,1)S(1)}, u32[]{:S(2)}, u32[]{:S(2)}) collective-permute-start(bf16[4,4,1,16,256]{4,3,1,0,2:T(8,128)(2,1)S(1)} %bitcast.688), channel_id=1, source_target_pairs={{1,0},{2,1},{3,2},{4,3},{5,4},{6,5},{7,6},{8,7},{9,8},{10,9},{11,1... | collective-permute-start | bytes 393224 | tf_op jit(solution)/shard_map/ppermute | solution.py:20
  75.0 7.1 %collective-permute-start = (bf16[4,4,1,16,256]{4,3,1,0,2:T(8,128)(2,1)S(1)}, bf16[4,4,1,16,256]{4,3,1,0,2:T(8,128)(2,1)S(1)}, u32[]{:S(2)}, u32[]{:S(2)}) collective-permute-start(bf16[4,4,1,16,256]{4,3,1,0,2:T(8,128)(2,1)S(1)} %bitcast.689), channel_id=1, source_target_pairs={{0,1},{1,2},{2,3},{3,4},{4,5},{5,6},{6,7},{7,8},{8,9},{9,10},{10,1... | collective-permute-start | bytes 393224 | tf_op jit(solution)/shard_map/ppermute | solution.py:19
  127.5 17.0 %copy-start.8 = (bf16[1,256,128]{1,0,2:T(2,128)(2,1)S(1)}, bf16[1,256,128]{1,0,2:T(2,128)(2,1)}, u32[]{:S(2)}) copy-start(bf16[1,256,128]{1,0,2:T(2,128)(2,1)} %get-tuple-element.49) | copy-start | bytes 196612
  127.5 18.2 %copy-start.7 = (bf16[1,256,128]{1,0,2:T(2,128)(2,1)S(1)}, bf16[1,256,128]{1,0,2:T(2,128)(2,1)}, u32[]{:S(2)}) copy-start(bf16[1,256,128]{1,0,2:T(2,128)(2,1)} %get-tuple-element.46) | copy-start | bytes 196612
  127.5 18.4 %copy-start.6 = (bf16[1,256,128]{1,0,2:T(2,128)(2,1)S(1)}, bf16[1,256,128]{1,0,2:T(2,128)(2,1)}, u32[]{:S(2)}) copy-start(bf16[1,256,128]{1,0,2:T(2,128)(2,1)} %get-tuple-element.45) | copy-start | bytes 196612
  127.5 18.5 %copy-start.5 = (bf16[1,256,128]{1,0,2:T(2,128)(2,1)S(1)}, bf16[1,256,128]{1,0,2:T(2,128)(2,1)}, u32[]{:S(2)}) copy-start(bf16[1,256,128]{1,0,2:T(2,128)(2,1)} %get-tuple-element.43) | copy-start | bytes 196612
  127.5 18.6 %copy-start.4 = (bf16[1,256,128]{1,0,2:T(2,128)(2,1)S(1)}, bf16[1,256,128]{1,0,2:T(2,128)(2,1)}, u32[]{:S(2)}) copy-start(bf16[1,256,128]{1,0,2:T(2,128)(2,1)} %get-tuple-element.42) | copy-start | bytes 196612
  127.5 18.8 %copy-start.3 = (bf16[1,256,128]{1,0,2:T(2,128)(2,1)S(1)}, bf16[1,256,128]{1,0,2:T(2,128)(2,1)}, u32[]{:S(2)}) copy-start(bf16[1,256,128]{1,0,2:T(2,128)(2,1)} %get-tuple-element.41) | copy-start | bytes 196612
  127.5 18.9 %copy-start.2 = (bf16[1,256,128]{1,0,2:T(2,128)(2,1)S(1)}, bf16[1,256,128]{1,0,2:T(2,128)(2,1)}, u32[]{:S(2)}) copy-start(bf16[1,256,128]{1,0,2:T(2,128)(2,1)} %get-tuple-element.40) | copy-start | bytes 196612
  127.5 23.2 %copy-start.9 = (bf16[4,2,1,16,256]{4,3,1,0,2:T(8,128)(2,1)S(1)}, bf16[4,2,1,16,256]{4,3,1,0,2:T(8,128)(2,1)}, u32[]{:S(2)}) copy-start(bf16[4,2,1,16,256]{4,3,1,0,2:T(8,128)(2,1)} %get-tuple-element.76) | copy-start | bytes 196612
  145.8 21.2 %copy-start.12 = (bf16[4,2,1,16,256]{4,3,1,0,2:T(8,128)(2,1)S(1)}, bf16[4,2,1,16,256]{4,3,1,0,2:T(8,128)(2,1)}, u32[]{:S(2)}) copy-start(bf16[4,2,1,16,256]{4,3,1,0,2:T(8,128)(2,1)} %get-tuple-element.67) | copy-start | bytes 196612
  146.1 22.0 %copy-start.11 = (bf16[4,2,1,16,256]{4,3,1,0,2:T(8,128)(2,1)S(1)}, bf16[4,2,1,16,256]{4,3,1,0,2:T(8,128)(2,1)}, u32[]{:S(2)}) copy-start(bf16[4,2,1,16,256]{4,3,1,0,2:T(8,128)(2,1)} %get-tuple-element.66) | copy-start | bytes 196612
  146.3 22.0 %copy-start.10 = (bf16[4,2,1,16,256]{4,3,1,0,2:T(8,128)(2,1)S(1)}, bf16[4,2,1,16,256]{4,3,1,0,2:T(8,128)(2,1)}, u32[]{:S(2)}) copy-start(bf16[4,2,1,16,256]{4,3,1,0,2:T(8,128)(2,1)} %get-tuple-element.65) | copy-start | bytes 196612
  146.6 21.9 %copy-start.13 = (bf16[4,2,1,16,256]{4,3,1,0,2:T(8,128)(2,1)S(1)}, bf16[4,2,1,16,256]{4,3,1,0,2:T(8,128)(2,1)}, u32[]{:S(2)}) copy-start(bf16[4,2,1,16,256]{4,3,1,0,2:T(8,128)(2,1)} %get-tuple-element.107) | copy-start | bytes 196612
  152.0 17.8 %copy-start.21 = (s32[4]{0:T(128)S(1)}, s32[4]{0:T(128)}, u32[]{:S(2)}) copy-start(s32[4]{0:T(128)} %copy-done.20) | copy-start | bytes 52
  157.0 118.6 %copy-start.19 = (f32[64]{0:T(128)S(1)}, f32[64]{0:T(128)}, u32[]{:S(2)}) copy-start(f32[64]{0:T(128)} %get-tuple-element.117) | copy-start | bytes 772
  158.0 118.3 %copy-start.14 = (bf16[4,2,1,16,128]{4,3,2,1,0:T(8,128)(2,1)S(1)}, bf16[4,2,1,16,128]{4,3,2,1,0:T(8,128)(2,1)}, u32[]{:S(2)}) copy-start(bf16[4,2,1,16,128]{4,3,2,1,0:T(8,128)(2,1)} %param.13) | copy-start | bytes 98308
  158.0 118.3 %copy-start.16 = (f32[128]{0:T(128)S(1)}, f32[128]{0:T(128)}, u32[]{:S(2)}) copy-start(f32[128]{0:T(128)} %param.11) | copy-start | bytes 1540
  158.0 118.3 %copy-start.17 = (f32[128]{0:T(128)S(1)}, f32[128]{0:T(128)}, u32[]{:S(2)}) copy-start(f32[128]{0:T(128)} %param.12) | copy-start | bytes 1540
  381.6 38.6 %all-to-all-start.1 = ((bf16[32,1,2,1,16,128]{5,4,2,3,1,0:T(8,128)(2,1)}), bf16[32,1,2,1,16,128]{5,4,2,3,1,0:T(8,128)(2,1)S(1)}, u32[]{:S(2)}, u32[]{:S(2)}) async-start(bf16[32,1,2,1,16,128]{5,4,2,3,1,0:T(8,128)(2,1)} %bitcast_select_fusion.1), calls=%async_computation.1 | async-start | bytes 524288 | tf_op jit(solution)/shard_map/all_to_all | solution.py:156
  386.6 171.2 %all-reduce.9.cloned.1.call-start = ((), (), s32[]{:S(2)}) async-start(), calls=%async_computation.4 | async-start | bytes 7077888
  420.1 0.7 copy-start.18
  420.2 214.6 %reduce-scatter.5.cloned.1.call-start = ((), (), s32[]{:S(2)}) async-start(), calls=%async_computation.5 | async-start | bytes 1880064
  420.9 6.0 collective-permute-start.3
  422.2 6.3 collective-permute-start.2
Sparse Core Ops, SparseCore 0:
  61.9 53.8 all-gather.2
  420.3 137.3 all-reduce.8
  561.1 73.6 reduce-scatter.4
where the time goes:
time: 645 us; the launch traced here: 643 us
  blocking collectives  239 us (37%)
  waiting for transfers between devices  232 us (36%)
  local copies, waits for them, and re-layouts  66.3 us (10%)
  matrix products  52.1 us (8%)
  starting transfers between devices  26.2 us (4%)
  between operations  15.4 us (2%)
  other arithmetic  12.1 us (2%)
    unnamed x5, waiting for transfers between devices  197 us
    psum x1, blocking collectives, body(): lax.psum((table_first, table_second), ('clips', 'slab'))  104 us
    psum x1, blocking collectives, body(): lax.psum((sum_grad, sum_cross, gain_part, bias_part), ('clips', 'slab'))  101 us
    all_gather x1, blocking collectives, body(): full_kernel = lax.all_gather(kernel, 'slab', axis=1, tiled=True)  33.9 us
    all_gather x1, waiting for transfers between devices, body(): full_kernel = lax.all_gather(full_kernel, 'clips', axis=0, tiled=True)  31.1 us
    slice x29, local copies, waits for them, and re-layouts, body(): kernel_taps[(forward_step_a * 3 + forward_step_b) * 3 + forward_step_c]  24.2 us
    dot_general x27, matrix products, body(): lax.dot_general(tap_rows, grad_flat, (((0,), (0,)), ((), ())), preferred_...  23.5 us
    dot_general x27, matrix products, body(): jnp.dot(tap_rows, kernel_taps[(forward_step_a * 3 + forward_step_b) * 3 +...  21.6 us
  transfers between devices with their start and end apart: 9, of which 6 were waited for; matrix products, arithmetic and copies ran while one was open for 9% of the time, Pallas kernels for 0%

commit v1 on v0

--- a/solution.py
+++ b/solution.py
@@ -1,3 +1,4 @@
+import functools
 import jax
 import jax.numpy as jnp
 from jax import lax
@@ -7,6 +8,16 @@
 TAPS = 27
 FB = 2
 BMAX = 3
+
+
+def run_the_flows(x_in, dev_axis, axis_k):
+    return jnp.concatenate(
+        lax.all_to_all(jnp.stack([x_in for _ in range(lax.axis_size(dev_axis))]), dev_axis, 0, 0),
+        axis=axis_k,
+    )
+
+
+manage_views = functools.partial(run_the_flows, dev_axis="clips", axis_k=0)
 
 
 def extended(array, sides, width):
@@ -49,7 +60,7 @@
         return jnp.sum((block_ends <= block_id[..., None]).astype(jnp.int32), axis=-1)
 
     full_kernel = lax.all_gather(kernel, "slab", axis=1, tiled=True)
-    full_kernel = lax.all_gather(full_kernel, "clips", axis=0, tiled=True)
+    full_kernel = manage_views(full_kernel)
     kernel_taps = full_kernel.reshape(in_channels, out_channels, TAPS).transpose(2, 0, 1)
 
     def group_sums(values):

time: 645 us -> 768 us (1.19)
  local copies, waits for them, and re-layouts: 66.3 us -> 218 us
  waiting for transfers between devices: 232 us -> 211 us
  matrix products: 52.1 us -> 41.9 us
    slice x29 -> x2, local copies, waits for them, and re-layouts: 24.2 us -> 161 us  [body(): kernel_taps[(forward_step_a * 3 + forward_step_b) * 3 + forward_step_c]]
    all_gather x1 -> x0, waiting for transfers between devices: 31.1 us -> none  [body(): full_kernel = lax.all_gather(full_kernel, 'clips', axis=0, tiled=True)]
    another operation x0 -> x2, local copies, waits for them, and re-layouts: none -> 22.5 us  [the longest x1 21.2 us: body(): full_kernel.reshape(in_channels, out_channels, TAPS).transpose(2, 0, 1)]
    all_to_all x0 -> x1, waiting for transfers between devices: none -> 11.2 us  [run_the_flows(): lax.all_to_all(jnp.stack([x_in for _ in range(lax.axis_size(dev_axis))]),...]
    dot_general x27, matrix products: 21.6 us -> 11.5 us  [body(): jnp.dot(tap_rows, kernel_taps[(forward_step_a * 3 + forward_step_b) * 3 +...]
    unnamed x5 -> x4, waiting for transfers between devices: 197 us -> 196 us
  transfers between devices with their start and end apart: 9 -> 9, of which waited for: 6 -> 6; matrix products, arithmetic and copies ran while one was open for 9% -> 7% of each run, Pallas kernels for 0% -> 0%
where the time goes in v1:
time: 768 us; the launch traced here: 767 us
  blocking collectives  234 us (30%)
  local copies, waits for them, and re-layouts  218 us (28%)
  waiting for transfers between devices  211 us (27%)
  matrix products  41.9 us (5%)
  starting transfers between devices  33.8 us (4%)
  between operations  15.6 us (2%)
  other arithmetic  12.1 us (2%)
    unnamed x4, waiting for transfers between devices  196 us
    slice x2, local copies, waits for them, and re-layouts, body(): kernel_taps[(forward_step_a * 3 + forward_step_b) * 3 + forward_step_c]  161 us
    psum x1, blocking collectives, body(): lax.psum((sum_grad, sum_cross, gain_part, bias_part), ('clips', 'slab'))  101 us
    psum x1, blocking collectives, body(): lax.psum((table_first, table_second), ('clips', 'slab'))  99.6 us
    all_gather x1, blocking collectives, body(): full_kernel = lax.all_gather(kernel, 'slab', axis=1, tiled=True)  33.9 us
    dot_general x27, matrix products, body(): lax.dot_general(tap_rows, grad_flat, (((0,), (0,)), ((), ())), preferred_...  23.3 us
    another operation x1, local copies, waits for them, and re-layouts, body(): full_kernel.reshape(in_channels, out_channels, TAPS).transpose(2, 0, 1)  21.2 us
  transfers between devices with their start and end apart: 9, of which 6 were waited for; matrix products, arithmetic and copies ran while one was open for 7% of the time, Pallas kernels for 0%

profile of v1, /device:TPU:2, one launch (start us, length us, event | category | flops | bytes accessed | tf_op | source)
XLA Modules:
  0.0 766.7 jit_solution(3550486191258491537)
XLA Ops:
  7.2 0.9 copy.37
  9.0 1.2 multiply_convert_fusion.2
  12.8 1.3 broadcast_compare_fusion
  16.4 1.1 fusion.36
  17.5 9.5 %all-to-all-start = ((bf16[32,1,4,1,16,256]{5,4,2,3,1,0:T(8,128)(2,1)}), bf16[32,1,4,1,16,256]{5,4,2,3,1,0:T(8,128)(2,1)S(1)}, u32[]{:S(2)}, u32[]{:S(2)}) async-start(bf16[32,1,4,1,16,256]{5,4,2,3,1,0:T(8,128)(2,1)} %fusion.36), calls=%async_computation | async-start | bytes 2097152 | tf_op jit(solution)/shard_map/all_to_all | solution.py:93
  29.2 33.9 %all-gather = bf16[16,216,8]{1,2,0:T(8,128)(2,1)S(1)} all-gather(bf16[1,216,8]{1,2,0:T(8,128)(2,1)S(1)} %bitcast.670), channel_id=1, replica_groups=mesh['clips'=32,'slab'=16] {'slab'}, dimensions={0}, use_global_device_ids=true | all-gather | bytes 58752 | tf_op jit(solution)/shard_map/all_gather | solution.py:62
  68.4 1.3 dynamic-slice.1
  71.0 1.3 stack.58
  72.3 7.4 all-to-all-start.1
  81.6 1.3 collective-permute-start.1
  82.9 4.7 collective-permute-start
  89.1 1.2 collective-permute-done
  91.9 1.0 fusion.161
  92.8 11.2 %all-to-all-done.1 = bf16[32,8,3456]{2,1,0:T(8,128)(2,1)S(1)} async-done(((bf16[32,8,3456]{2,1,0:T(8,128)(2,1)}), bf16[32,8,3456]{2,1,0:T(8,128)(2,1)S(1)}, u32[]{:S(2)}, u32[]{:S(2)}) %all-to-all-start.1) | async-done | bytes 1769504 | tf_op jit(solution)/shard_map/all_to_all | solution.py:15
  104.0 21.2 %reshape_reshape.9 = bf16[256,128,27]{2,1,0:T(8,128)(2,1)} reshape(bf16[32,8,3456]{2,1,0:T(8,128)(2,1)S(1)} %all-to-all-done.1) | data formatting | bytes 3538944 | tf_op jit(solution)/shard_map/reshape;reshape | solution.py:64
  125.2 114.4 %slice_reduce_fusion.1 = (bf16[256,128]{1,0:T(8,128)(2,1)S(1)}, bf16[256,128]{1,0:T(8,128)(2,1)S(1)}, bf16[256,128]{1,0:T(8,128)(2,1)S(1)}, bf16[256,128]{1,0:T(...) fusion(bf16[27,256,128]{0,2,1:T(8,128)(2,1)} %bitcast.600), kind=kLoop, calls=%fused_computation.13 | loop fusion | bytes 2490368 | tf_op jit(solution)/shard_map/slice | solution.py:118
  239.6 46.5 %slice_reduce_fusion.19 = (bf16[256,128]{1,0:T(8,128)(2,1)S(1)}, bf16[256,128]{1,0:T(8,128)(2,1)S(1)}, bf16[256,128]{1,0:T(8,128)(2,1)S(1)}, bf16[256,128]{1,0:T...) fusion(bf16[27,256,128]{0,2,1:T(8,128)(2,1)} %bitcast.601), kind=kLoop, calls=%fused_computation.31 | loop fusion | bytes 1048576 | tf_op jit(solution)/shard_map/slice | solution.py:118
  287.2 1.0 convolution_add_fusion.44
  288.2 1.0 convolution_add_fusion.43
  289.2 1.0 convolution_add_fusion.42
  290.2 1.0 convolution_add_fusion.41
  291.2 1.0 convolution_add_fusion.40
  292.1 1.0 convolution_add_fusion.39
  293.2 1.0 fusion.35
  294.2 1.0 convolution_add_fusion.37
  295.2 1.0 fusion.34
  300.8 99.6 %all-reduce.6 = (f32[64,16]{0,1:T(8,128)S(1)}, f32[64,16]{0,1:T(8,128)S(1)}) all-reduce(f32[64,16]{0,1:T(8,128)S(1)} %fusion.97, f32[64,16]{0,1:T(8,128)S(1)} %fusion.98), channel_id=1, replica_groups=mesh['clips'=32,'slab'=16] {'clips','slab'}, use_global_device_ids=true, to_apply=%region_7.8 | all-reduce | flops 2048 | bytes 16384 | tf_op jit(solution)/shard_map/psum | solution.py:130
  402.7 100.8 %all-reduce.5 = (f32[64,16]{0,1:T(8,128)S(1)}, f32[64,16]{0,1:T(8,128)S(1)}, f32[128]{0:T(128)}, f32[128]{0:T(128)}) all-reduce(f32[64,16]{0,1:T(8,128)S(1)} %fusion.95, f32[64,16]{0,1:T(8,128)S(1)} %fusion.96, f32[128]{0:T(128)S(1)} %get-tuple-element.52, ...), channel_id=1, replica_groups=mesh['clips'=32,'slab'=16] {'clips','slab'}, use_global_device_ids=true, to_apply=%region_13.14 | all-reduce | flops 2304 | bytes 18432 | tf_op jit(solution)/shard_map/psum | solution.py:149
  504.3 0.9 fusion.30
  506.6 5.0 all-to-all-start.2
  512.4 0.9 fusion.28
  513.3 0.9 fusion.27
  514.2 0.9 fusion.26
  515.0 0.9 fusion.25
  515.9 0.9 fusion.24
  516.8 0.9 fusion.23
  517.6 0.9 fusion.22
  518.5 0.9 fusion.21
  519.3 0.9 fusion.20
  520.2 0.9 fusion.19
  521.1 0.9 fusion.18
  522.0 0.9 fusion.17
  522.8 0.9 fusion.16
  523.7 0.9 fusion.15
  524.6 0.9 fusion.14
  525.4 0.9 fusion.13
  526.3 0.9 fusion.12
  527.2 0.9 fusion.11
  528.0 0.9 fusion.10
  528.9 0.9 fusion.9
  529.7 0.9 fusion.8
  530.6 0.9 fusion.7
  531.5 0.9 fusion.6
  532.3 0.9 fusion.5
  533.2 0.9 fusion.4
  534.1 6.0 copy.43
  540.1 4.9 reshape.1309
  545.7 1.3 collective-permute-start.3
  547.0 4.5 collective-permute-start.2
  551.7 1.6 collective-permute-done.2
  558.3 122.9 %all-reduce.9.cloned.1.call-done = f32[256,3456]{0,1:T(8,128)} async-done(((f32[256,3456]{0,1:T(8,128)}), f32[256,3456]{0,1:T(8,128)}) %all-reduce.9.cloned.1.call-update) | async-done | bytes 3538960
  681.3 3.2 constant_dynamic-slice_fusion
  685.3 73.0 %reduce-scatter.5.cloned.1.call-done = f32[8,216]{0,1:T(8,128)} async-done(((f32[8,3456]{0,1:T(8,128)}), f32[8,216]{0,1:T(8,128)}) %reduce-scatter.5.cloned.1.call-update) | async-done | bytes 6928
  758.3 1.6 copy.45
  (193 shorter events, 36.0 us)
Async XLA Ops:
  15.6 13.6 %copy-start.18 = (bf16[8,216]{1,0:T(8,128)(2,1)S(1)}, bf16[8,216]{1,0:T(8,128)(2,1)}, u32[]{:S(2)}) copy-start(bf16[8,216]{1,0:T(8,128)(2,1)} %param.10) | copy-start | bytes 10372
  15.7 47.5 %copy-start.1 = (s32[64]{0:T(128)S(1)}, s32[64]{0:T(128)}, u32[]{:S(2)}) copy-start(s32[64]{0:T(128)} %param.8) | copy-start | bytes 772
  16.4 49.7 %copy-start = (s32[32]{0:T(128)S(1)}, s32[32]{0:T(128)}, u32[]{:S(2)}) copy-start(s32[32]{0:T(128)} %param.9) | copy-start | bytes 388
  17.5 53.4 %all-to-all-start = ((bf16[32,1,4,1,16,256]{5,4,2,3,1,0:T(8,128)(2,1)}), bf16[32,1,4,1,16,256]{5,4,2,3,1,0:T(8,128)(2,1)S(1)}, u32[]{:S(2)}, u32[]{:S(2)}) async-start(bf16[32,1,4,1,16,256]{5,4,2,3,1,0:T(8,128)(2,1)} %fusion.36), calls=%async_computation | async-start | bytes 2097152 | tf_op jit(solution)/shard_map/all_to_all | solution.py:93
  28.5 43.9 %copy-start.23 = (s32[4]{0:T(128)}, s32[4]{0:T(128)S(1)}, u32[]{:S(2)}) copy-start(s32[4]{0:T(128)S(1)} %convert_reduce_fusion.1) | copy-start | bytes 52
  72.3 31.7 %all-to-all-start.1 = ((bf16[32,8,3456]{2,1,0:T(8,128)(2,1)}), bf16[32,8,3456]{2,1,0:T(8,128)(2,1)S(1)}, u32[]{:S(2)}, u32[]{:S(2)}) async-start(bf16[32,8,3456]{2,1,0:T(8,128)(2,1)} %stack.58), calls=%async_computation.1 | async-start | bytes 3538944 | tf_op jit(solution)/shard_map/all_to_all | solution.py:15
  81.6 7.4 collective-permute-start.1
  82.9 7.3 collective-permute-start
  239.6 46.6 %copy-start.4 = (bf16[4,2,1,16,256]{4,3,1,0,2:T(8,128)(2,1)S(1)}, bf16[4,2,1,16,256]{4,3,1,0,2:T(8,128)(2,1)}, u32[]{:S(2)}) copy-start(bf16[4,2,1,16,256]{4,3,1,0,2:T(8,128)(2,1)} %get-tuple-element.82) | copy-start | bytes 196612
  239.6 46.8 %copy-start.3 = (bf16[4,2,1,16,256]{4,3,1,0,2:T(8,128)(2,1)S(1)}, bf16[4,2,1,16,256]{4,3,1,0,2:T(8,128)(2,1)}, u32[]{:S(2)}) copy-start(bf16[4,2,1,16,256]{4,3,1,0,2:T(8,128)(2,1)} %get-tuple-element.68) | copy-start | bytes 196612
  239.6 46.9 %copy-start.2 = (bf16[4,2,1,16,256]{4,3,1,0,2:T(8,128)(2,1)S(1)}, bf16[4,2,1,16,256]{4,3,1,0,2:T(8,128)(2,1)}, u32[]{:S(2)}) copy-start(bf16[4,2,1,16,256]{4,3,1,0,2:T(8,128)(2,1)} %get-tuple-element.70) | copy-start | bytes 196612
  286.1 10.1 %copy-start.13 = (bf16[4,2,1,16,256]{4,3,1,0,2:T(8,128)(2,1)S(1)}, bf16[4,2,1,16,256]{4,3,1,0,2:T(8,128)(2,1)}, u32[]{:S(2)}) copy-start(bf16[4,2,1,16,256]{4,3,1,0,2:T(8,128)(2,1)} %get-tuple-element.73) | copy-start | bytes 196612
  286.1 10.2 %copy-start.16 = (bf16[4,2,1,16,256]{4,3,1,0,2:T(8,128)(2,1)S(1)}, bf16[4,2,1,16,256]{4,3,1,0,2:T(8,128)(2,1)}, u32[]{:S(2)}) copy-start(bf16[4,2,1,16,256]{4,3,1,0,2:T(8,128)(2,1)} %get-tuple-element.111) | copy-start | bytes 196612
  286.1 10.4 %copy-start.12 = (bf16[4,2,1,16,256]{4,3,1,0,2:T(8,128)(2,1)S(1)}, bf16[4,2,1,16,256]{4,3,1,0,2:T(8,128)(2,1)}, u32[]{:S(2)}) copy-start(bf16[4,2,1,16,256]{4,3,1,0,2:T(8,128)(2,1)} %get-tuple-element.72) | copy-start | bytes 196612
  286.1 10.5 %copy-start.11 = (bf16[4,2,1,16,256]{4,3,1,0,2:T(8,128)(2,1)S(1)}, bf16[4,2,1,16,256]{4,3,1,0,2:T(8,128)(2,1)}, u32[]{:S(2)}) copy-start(bf16[4,2,1,16,256]{4,3,1,0,2:T(8,128)(2,1)} %get-tuple-element.71) | copy-start | bytes 196612
  286.1 10.7 %copy-start.7 = (bf16[4,2,1,16,256]{4,3,1,0,2:T(8,128)(2,1)S(1)}, bf16[4,2,1,16,256]{4,3,1,0,2:T(8,128)(2,1)}, u32[]{:S(2)}) copy-start(bf16[4,2,1,16,256]{4,3,1,0,2:T(8,128)(2,1)} %get-tuple-element.108) | copy-start | bytes 196612
  286.2 10.8 %copy-start.10 = (bf16[4,2,1,16,256]{4,3,1,0,2:T(8,128)(2,1)S(1)}, bf16[4,2,1,16,256]{4,3,1,0,2:T(8,128)(2,1)}, u32[]{:S(2)}) copy-start(bf16[4,2,1,16,256]{4,3,1,0,2:T(8,128)(2,1)} %get-tuple-element.69) | copy-start | bytes 196612
  286.2 11.0 %copy-start.5 = (bf16[4,2,1,16,256]{4,3,1,0,2:T(8,128)(2,1)S(1)}, bf16[4,2,1,16,256]{4,3,1,0,2:T(8,128)(2,1)}, u32[]{:S(2)}) copy-start(bf16[4,2,1,16,256]{4,3,1,0,2:T(8,128)(2,1)} %get-tuple-element.113) | copy-start | bytes 196612
  286.2 11.1 %copy-start.9 = (bf16[4,2,1,16,256]{4,3,1,0,2:T(8,128)(2,1)S(1)}, bf16[4,2,1,16,256]{4,3,1,0,2:T(8,128)(2,1)}, u32[]{:S(2)}) copy-start(bf16[4,2,1,16,256]{4,3,1,0,2:T(8,128)(2,1)} %get-tuple-element.67) | copy-start | bytes 196612
  286.2 11.3 %copy-start.14 = (bf16[4,2,1,16,256]{4,3,1,0,2:T(8,128)(2,1)S(1)}, bf16[4,2,1,16,256]{4,3,1,0,2:T(8,128)(2,1)}, u32[]{:S(2)}) copy-start(bf16[4,2,1,16,256]{4,3,1,0,2:T(8,128)(2,1)} %get-tuple-element.110) | copy-start | bytes 196612
  286.2 11.4 %copy-start.8 = (bf16[4,2,1,16,256]{4,3,1,0,2:T(8,128)(2,1)S(1)}, bf16[4,2,1,16,256]{4,3,1,0,2:T(8,128)(2,1)}, u32[]{:S(2)}) copy-start(bf16[4,2,1,16,256]{4,3,1,0,2:T(8,128)(2,1)} %get-tuple-element.66) | copy-start | bytes 196612
  286.2 11.6 %copy-start.6 = (bf16[4,2,1,16,256]{4,3,1,0,2:T(8,128)(2,1)S(1)}, bf16[4,2,1,16,256]{4,3,1,0,2:T(8,128)(2,1)}, u32[]{:S(2)}) copy-start(bf16[4,2,1,16,256]{4,3,1,0,2:T(8,128)(2,1)} %get-tuple-element.65) | copy-start | bytes 196612
  286.2 11.7 %copy-start.15 = (bf16[4,2,1,16,256]{4,3,1,0,2:T(8,128)(2,1)S(1)}, bf16[4,2,1,16,256]{4,3,1,0,2:T(8,128)(2,1)}, u32[]{:S(2)}) copy-start(bf16[4,2,1,16,256]{4,3,1,0,2:T(8,128)(2,1)} %get-tuple-element.107) | copy-start | bytes 196612
  288.2 11.1 %copy-start.24 = (s32[4]{0:T(128)S(1)}, s32[4]{0:T(128)}, u32[]{:S(2)}) copy-start(s32[4]{0:T(128)} %copy-done.23) | copy-start | bytes 52
  293.1 107.3 %copy-start.22 = (f32[64]{0:T(128)S(1)}, f32[64]{0:T(128)}, u32[]{:S(2)}) copy-start(f32[64]{0:T(128)} %get-tuple-element.117) | copy-start | bytes 772
  294.2 107.0 %copy-start.17 = (bf16[4,2,1,16,128]{4,3,2,1,0:T(8,128)(2,1)S(1)}, bf16[4,2,1,16,128]{4,3,2,1,0:T(8,128)(2,1)}, u32[]{:S(2)}) copy-start(bf16[4,2,1,16,128]{4,3,2,1,0:T(8,128)(2,1)} %param.13) | copy-start | bytes 98308
  294.2 107.0 %copy-start.19 = (f32[128]{0:T(128)S(1)}, f32[128]{0:T(128)}, u32[]{:S(2)}) copy-start(f32[128]{0:T(128)} %param.11) | copy-start | bytes 1540
  294.2 107.0 %copy-start.20 = (f32[128]{0:T(128)S(1)}, f32[128]{0:T(128)}, u32[]{:S(2)}) copy-start(f32[128]{0:T(128)} %param.12) | copy-start | bytes 1540
  506.6 38.5 %all-to-all-start.2 = ((bf16[32,1,2,1,16,128]{5,4,2,3,1,0:T(8,128)(2,1)}), bf16[32,1,2,1,16,128]{5,4,2,3,1,0:T(8,128)(2,1)S(1)}, u32[]{:S(2)}, u32[]{:S(2)}) async-start(bf16[32,1,2,1,16,128]{5,4,2,3,1,0:T(8,128)(2,1)} %bitcast_select_fusion.1), calls=%async_computation.2 | async-start | bytes 524288 | tf_op jit(solution)/shard_map/all_to_all | solution.py:167
  511.5 169.7 %all-reduce.9.cloned.1.call-start = ((), (), s32[]{:S(2)}) async-start(), calls=%async_computation.4 | async-start | bytes 7077888
  544.9 0.7 copy-start.21
  545.0 213.4 %reduce-scatter.5.cloned.1.call-start = ((), (), s32[]{:S(2)}) async-start(), calls=%async_computation.5 | async-start | bytes 1880064
  545.7 6.0 collective-permute-start.3
  547.0 6.3 collective-permute-start.2
Sparse Core Ops, SparseCore 0:
  545.1 136.1 all-reduce.8
  684.6 73.6 reduce-scatter.4
